TPU v7x, 32 devices: a whole 2x2x4 slice. The times are simulated.
32 devices in a mesh: groups: 2 (over y), wide: 16 (over z, x, core).
Axes of the slice: x: 2, y: 2, z: 4, core: 2. Of those that a mesh axis runs over, the one named last changes fastest.
Arguments:
- fields: bfloat16 [32, 512], P(('groups', 'wide')), parts along dimension 0, may hold values from -6 to 6
- chol: bfloat16 [512, 1024, 1024], P(None, 'wide'), may hold values from -0.01171875 to 0.01171875
- orbitals: bfloat16 [32, 1024, 256], P(('groups', 'wide')), parts along dimension 0, may hold values from -6 to 6
- trial: bfloat16 [1024, 256], replicated, may hold values from -0.5 to 0.5
Outputs:
- new_orbitals: bfloat16 [32, 1024, 256], P(('groups', 'wide')), parts along dimension 0
- force_bias: float32 [32, 2, 512], P(('groups', 'wide')), parts along dimension 0
There are 2 independent parts, one for each index of `groups`. A program takes and returns all parts, laid end to end along the dimension named above; an argument that names none is the same for every part. Nothing has to cross between parts.
All inputs are finite; a program needn't handle non-finite values.
Results may differ from a plain program's by a relative error of at most 0.0075.
Values may be sent and summed in bfloat16 or wider, within the bound.
No kernel may reach another device: no remote copies, remote signals or barrier semaphores. Data moves between devices by JAX's collectives and lax.ppermute only.
A program may use at most 192 MiB of HBM per device.

v0:
```python
import jax
import jax.numpy as jnp
from jax import lax
from jax.sharding import PartitionSpec as P

TAYLOR = 4


def per_device(fields, chol, orbitals, trial):
    all_fields = lax.all_gather(fields, "wide", axis=0, tiled=True)
    vectors, rows, width = chol.shape
    chol_flat = chol.reshape(vectors, rows * width)
    generator = jnp.dot(all_fields, chol_flat, preferred_element_type=jnp.float32).astype(
        jnp.bfloat16
    )
    generator = generator.reshape(all_fields.shape[0], rows, width)
    owned = lax.all_to_all(generator, "wide", split_axis=0, concat_axis=1, tiled=True)
    nocc = orbitals.shape[2] // 2
    walk_local = orbitals.shape[0]
    gen_walker = owned[0]
    total = orbitals[0].astype(jnp.float32)
    operand = orbitals[0]
    for order in range(1, TAYLOR + 1):
        product = jnp.dot(gen_walker, operand, preferred_element_type=jnp.float32)
        term = jnp.concatenate([-product[:, nocc:], product[:, :nocc]], axis=1) / order
        total = total + term
        if order < TAYLOR:
            operand = term.astype(jnp.bfloat16)
    fresh_list = [total.astype(jnp.bfloat16)]
    new_orbitals = jnp.stack(fresh_list, axis=0)
    trial_real = trial[:, :nocc].T
    trial_imag = trial[:, nocc:].T
    mixer = jnp.concatenate(
        [
            jnp.concatenate([trial_real, -trial_imag], axis=1),
            jnp.concatenate([trial_imag, trial_real], axis=1),
        ],
        axis=0,
    )
    orbital_rows = lax.all_to_all(new_orbitals, "wide", split_axis=1, concat_axis=0, tiled=True)
    count = orbital_rows.shape[0]
    flat_rows = orbital_rows.reshape(count * rows, 2 * nocc)
    tile_green = jnp.dot(flat_rows, mixer, preferred_element_type=jnp.float32).astype(jnp.bfloat16)
    tile_green = tile_green.reshape(count, rows, 2 * width)
    all_walk = tile_green.shape[0]
    tile_green = (
        tile_green.reshape(all_walk, rows, 2, width)
        .transpose(0, 2, 1, 3)
        .reshape(all_walk * 2, rows * width)
    )
    partial_value = jnp.dot(tile_green, chol_flat.T, preferred_element_type=jnp.float32).reshape(
        all_walk, 2, vectors
    )
    summed = lax.psum(partial_value, "wide")
    force_bias = lax.dynamic_slice_in_dim(
        summed, lax.axis_index("wide") * walk_local, walk_local, 0
    )
    return (new_orbitals, force_bias)


def solution(mesh):
    in_specs = (
        P(("groups", "wide"), None),
        P(None, "wide", None),
        P(("groups", "wide"), None, None),
        P(),
    )
    out_specs = (P(("groups", "wide"), None, None), P(("groups", "wide"), None, None))
    return jax.shard_map(
        per_device, mesh=mesh, in_specs=in_specs, out_specs=out_specs, check_vma=False
    )
```

profile of v0, /device:TPU:8, one launch (start us, length us, event | category | flops | bytes accessed | tf_op | source)
XLA Modules:
  0.0 381.3 jit_solution(17390543338026890626)
XLA Ops:
  7.2 58.5 %copy.31 = bf16[64,8,64,1024]{3,1,2,0:T(8,128)(2,1)} copy(bf16[64,8,64,1024]{3,2,1,0:T(8,128)(2,1)} %bitcast.19) | data formatting | bytes 134217728
  65.7 18.9 %all-gather = bf16[16,1,512]{2,1,0:T(2,128)(2,1)S(1)} all-gather(bf16[1,1,512]{2,1,0:T(2,128)(2,1)S(1)} %bitcast.65), channel_id=1, replica_groups=mesh['groups'=2,'wide'=16] {'wide'}, dimensions={0}, use_global_device_ids=true | all-gather | bytes 17408 | tf_op jit(solution)/shard_map/all_gather | solution.py:10
  84.6 22.8 %convolution_convert_fusion = bf16[16,65536]{1,0:T(8,128)(2,1)S(1)} fusion(bf16[512,65536]{1,0:T(8,128)(2,1)} %bitcast.20, bf16[16,1,512]{2,1,0:T(2,128)(2,1)S(1)} %all-gather), kind=kOutput, calls=%fused_computation | convolution fusion | flops 1074790400 | bytes 69222400 | tf_op jit(solution)/shard_map/dot_general | solution.py:13
  107.4 2.5 copy.32
  109.9 6.9 %all-to-all-start = ((bf16[16,64,1024]{2,1,0:T(8,128)(2,1)}), bf16[16,64,1024]{2,1,0:T(8,128)(2,1)S(1)}, u32[]{:S(2)}, u32[]{:S(2)}) async-start(bf16[16,64,1024]{2,1,0:T(8,128)(2,1)} %bitcast.62), calls=%async_computation | async-start | bytes 4194304 | tf_op jit(solution)/shard_map/all_to_all | solution.py:17
  117.0 45.6 %all-to-all-done = bf16[16,64,1024]{2,1,0:T(8,128)(2,1)S(1)} async-done(((bf16[16,64,1024]{2,1,0:T(8,128)(2,1)}), bf16[16,64,1024]{2,1,0:T(8,128)(2,1)S(1)}, u32[]{:S(2)}, u32[]{:S(2)}) %all-to-all-start) | async-done | bytes 2097184 | tf_op jit(solution)/shard_map/all_to_all | solution.py:17
  162.7 0.8 fusion.34
  163.6 0.7 fusion.28
  164.5 0.7 fusion.25
  165.4 0.7 fusion.23
  166.2 0.6 fusion.13
  166.8 0.9 copy.23
  168.2 3.8 %reduce = bf16[1024,256]{1,0:T(8,128)(2,1)S(1)} reduce(bf16[1024,1,256]{2,1,0:T(2,128)(2,1)S(1)} %bitcast.63, bf16[]{:T(256)} %broadcast.24), dimensions={1}, to_apply=%bitcast.50.reduce_sub_computation | reduce | bytes 1048578
  172.0 0.9 reshape.121
  172.9 6.4 %all-to-all-start.1 = ((bf16[16,2,8192]{2,1,0:T(2,128)(2,1)}), bf16[16,2,8192]{2,1,0:T(2,128)(2,1)S(1)}, u32[]{:S(2)}, u32[]{:S(2)}) async-start(bf16[16,2,8192]{2,1,0:T(2,128)(2,1)} %reshape.121), calls=%async_computation.1 | async-start | bytes 1048576 | tf_op jit(solution)/shard_map/all_to_all | solution.py:40
  179.4 13.3 %all-to-all-done.1 = bf16[16,2,8192]{2,1,0:T(2,128)(2,1)S(1)} async-done(((bf16[16,2,8192]{2,1,0:T(2,128)(2,1)}), bf16[16,2,8192]{2,1,0:T(2,128)(2,1)S(1)}, u32[]{:S(2)}, u32[]{:S(2)}) %all-to-all-start.1) | async-done | bytes 524320 | tf_op jit(solution)/shard_map/all_to_all | solution.py:40
  192.8 0.5 reshape.122
  193.3 3.3 convolution_convert_fusion.1
  196.6 7.8 %reshape_reshape.3 = bf16[16,64,2,1024]{3,2,1,0:T(2,128)(2,1)} reshape(bf16[1024,2048]{1,0:T(8,128)(2,1)} %convolution_convert_fusion.1) | data formatting | bytes 8388608 | tf_op jit(solution)/shard_map/reshape;reshape | solution.py:47
  204.3 80.0 %fusion.5 = f32[16,2,512]{2,0,1:T(8,128)} fusion(bf16[512,64,1024]{2,1,0:T(8,128)(2,1)} %param.5, bf16[16,64,2,1024]{3,2,1,0:T(2,128)(2,1)} %reshape_reshape.3), kind=kOutput, calls=%fused_computation.7 | convolution fusion | flops 2147483648 | bytes 71368704 | tf_op jit(solution)/shard_map/dot_general | solution.py:51
  284.3 1.0 copy.26
  285.3 87.8 %all-reduce.2.cloned.1.call-done = f32[16,2,512]{2,0,1:T(8,128)} async-done(((f32[16,2,512]{2,0,1:T(8,128)}), f32[16,2,512]{2,0,1:T(8,128)}) %all-reduce.2.cloned.1.call-update) | async-done | bytes 65552 | tf_op jit(solution)/shard_map/psum | solution.py:54
  373.1 0.8 constant_dynamic-slice_fusion
  373.9 0.6 copy.27
  (17 shorter events, 1.4 us)
Async XLA Ops:
  7.2 58.6 %copy-start.2 = (bf16[1,512]{1,0:T(2,128)(2,1)S(1)}, bf16[1,512]{1,0:T(2,128)(2,1)}, u32[]{:S(2)}) copy-start(bf16[1,512]{1,0:T(2,128)(2,1)} %param.4) | copy-start | bytes 3076
  109.9 6.9 %copy-start = (bf16[1,1024,256]{2,1,0:T(8,128)(2,1)S(1)}, bf16[1,1024,256]{2,1,0:T(8,128)(2,1)}, u32[]{:S(2)}) copy-start(bf16[1,1024,256]{2,1,0:T(8,128)(2,1)} %param.6) | copy-start | bytes 1572868
  109.9 52.8 %all-to-all-start = ((bf16[16,64,1024]{2,1,0:T(8,128)(2,1)}), bf16[16,64,1024]{2,1,0:T(8,128)(2,1)S(1)}, u32[]{:S(2)}, u32[]{:S(2)}) async-start(bf16[16,64,1024]{2,1,0:T(8,128)(2,1)} %bitcast.62), calls=%async_computation | async-start | bytes 4194304 | tf_op jit(solution)/shard_map/all_to_all | solution.py:17
  167.6 11.7 %copy-start.1 = (bf16[1024,256]{1,0:T(8,128)(2,1)S(1)}, bf16[1024,256]{1,0:T(8,128)(2,1)}, u32[]{:S(2)}) copy-start(bf16[1024,256]{1,0:T(8,128)(2,1)} %param.7) | copy-start | bytes 1572868
  172.9 19.8 %all-to-all-start.1 = ((bf16[16,2,8192]{2,1,0:T(2,128)(2,1)}), bf16[16,2,8192]{2,1,0:T(2,128)(2,1)S(1)}, u32[]{:S(2)}, u32[]{:S(2)}) async-start(bf16[16,2,8192]{2,1,0:T(2,128)(2,1)} %reshape.121), calls=%async_computation.1 | async-start | bytes 1048576 | tf_op jit(solution)/shard_map/all_to_all | solution.py:40
  179.3 193.8 %all-reduce.2.cloned.1.call-start = ((), (), s32[]{:S(2)}) async-start(), calls=%async_computation.2 | async-start | bytes 131072 | tf_op jit(solution)/shard_map/psum | solution.py:54
Sparse Core Ops, SparseCore 0:
  284.4 88.6 all-reduce.1
where the time goes:
time: 382 us; the launch traced here: 381 us
  waiting for transfers between devices  147 us (38%)
  matrix products  109 us (29%)
  local copies, waits for them, and re-layouts  74.3 us (19%)
  blocking collectives  18.9 us (5%)
  between operations  14.2 us (4%)
  starting transfers between devices  13.3 us (3%)
  other arithmetic  4.9 us (1%)
    psum x1, waiting for transfers between devices, per_device(): summed = lax.psum(partial_value, 'wide')  87.8 us
    dot_general x1, matrix products, per_device(): jnp.dot(tile_green, chol_flat.T, preferred_element_type=jnp.float32)  80 us
    unnamed x14, local copies, waits for them, and re-layouts  64.8 us
    all_to_all x1, waiting for transfers between devices, per_device(): lax.all_to_all(generator, 'wide', split_axis=0, concat_axis=1, tiled=True)  45.6 us
    dot_general x1, matrix products, per_device(): jnp.dot(all_fields, chol_flat, preferred_element_type=jnp.float32)  22.8 us
    all_gather x1, blocking collectives, per_device(): all_fields = lax.all_gather(fields, 'wide', axis=0, tiled=True)  18.9 us
    all_to_all x1, waiting for transfers between devices, per_device(): lax.all_to_all(new_orbitals, 'wide', split_axis=1, concat_axis=0, tiled=T...  13.3 us
    another operation x1, local copies, waits for them, and re-layouts, per_device(): tile_green.reshape(all_walk, rows, 2, width).transpose(0, 2, 1, 3)  7.78 us
  transfers between devices with their start and end apart: 3, of which 3 were waited for; matrix products, arithmetic and copies ran while one was open for 0% of the time, Pallas kernels for 0%

commit v1 on v0

--- a/solution.py
+++ b/solution.py
@@ -51,7 +51,7 @@
     partial_value = jnp.dot(tile_green, chol_flat.T, preferred_element_type=jnp.float32).reshape(
         all_walk, 2, vectors
     )
-    summed = lax.psum(partial_value, "wide")
+    summed = jnp.sum(lax.all_gather(partial_value, "wide"), axis=0)
     force_bias = lax.dynamic_slice_in_dim(
         summed, lax.axis_index("wide") * walk_local, walk_local, 0
     )

time: 382 us -> 333 us (0.87)
  waiting for transfers between devices: 147 us -> 94.9 us
    psum x1 -> x0, waiting for transfers between devices: 87.8 us -> none  [per_device(): summed = lax.psum(partial_value, 'wide')]
    all_gather x0 -> x1, waiting for transfers between devices: none -> 35.9 us  [per_device(): summed = jnp.sum(lax.all_gather(partial_value, 'wide'), axis=0)]
where the time goes in v1:
time: 333 us; the launch traced here: 330 us
  matrix products  109 us (33%)
  waiting for transfers between devices  94.9 us (28%)
  local copies, waits for them, and re-layouts  73.5 us (22%)
  blocking collectives  18.9 us (6%)
  between operations  14.2 us (4%)
  starting transfers between devices  13.3 us (4%)
  other arithmetic  6.23 us (2%)
    dot_general x1, matrix products, per_device(): jnp.dot(tile_green, chol_flat.T, preferred_element_type=jnp.float32)  80 us
    unnamed x14, local copies, waits for them, and re-layouts  64.8 us
    all_to_all x1, waiting for transfers between devices, per_device(): lax.all_to_all(generator, 'wide', split_axis=0, concat_axis=1, tiled=True)  45.6 us
    all_gather x1, waiting for transfers between devices, per_device(): summed = jnp.sum(lax.all_gather(partial_value, 'wide'), axis=0)  35.9 us
    dot_general x1, matrix products, per_device(): jnp.dot(all_fields, chol_flat, preferred_element_type=jnp.float32)  22.8 us
    all_gather x1, blocking collectives, per_device(): all_fields = lax.all_gather(fields, 'wide', axis=0, tiled=True)  18.9 us
    all_to_all x1, waiting for transfers between devices, per_device(): lax.all_to_all(new_orbitals, 'wide', split_axis=1, concat_axis=0, tiled=T...  13.3 us
    another operation x1, local copies, waits for them, and re-layouts, per_device(): tile_green.reshape(all_walk, rows, 2, width).transpose(0, 2, 1, 3)  7.78 us
  transfers between devices with their start and end apart: 3, of which 3 were waited for; matrix products, arithmetic and copies ran while one was open for 0% of the time, Pallas kernels for 0%

profile of v1, /device:TPU:8, one launch (start us, length us, event | category | flops | bytes accessed | tf_op | source)
XLA Modules:
  0.0 330.0 jit_solution(16870788138892243443)
XLA Ops:
  7.2 58.5 %copy.29 = bf16[64,8,64,1024]{3,1,2,0:T(8,128)(2,1)} copy(bf16[64,8,64,1024]{3,2,1,0:T(8,128)(2,1)} %bitcast.20) | data formatting | bytes 134217728
  65.7 18.9 %all-gather.1 = bf16[16,1,512]{2,1,0:T(2,128)(2,1)S(1)} all-gather(bf16[1,1,512]{2,1,0:T(2,128)(2,1)S(1)} %bitcast.67), channel_id=1, replica_groups=mesh['groups'=2,'wide'=16] {'wide'}, dimensions={0}, use_global_device_ids=true | all-gather | bytes 17408 | tf_op jit(solution)/shard_map/all_gather | solution.py:10
  84.6 22.8 %convolution_convert_fusion = bf16[16,65536]{1,0:T(8,128)(2,1)S(1)} fusion(bf16[512,65536]{1,0:T(8,128)(2,1)} %bitcast.21, bf16[16,1,512]{2,1,0:T(2,128)(2,1)S(1)} %all-gather.1), kind=kOutput, calls=%fused_computation | convolution fusion | flops 1074790400 | bytes 69222400 | tf_op jit(solution)/shard_map/dot_general | solution.py:13
  107.4 2.5 copy.30
  109.9 6.9 %all-to-all-start = ((bf16[16,64,1024]{2,1,0:T(8,128)(2,1)}), bf16[16,64,1024]{2,1,0:T(8,128)(2,1)S(1)}, u32[]{:S(2)}, u32[]{:S(2)}) async-start(bf16[16,64,1024]{2,1,0:T(8,128)(2,1)} %bitcast.63), calls=%async_computation | async-start | bytes 4194304 | tf_op jit(solution)/shard_map/all_to_all | solution.py:17
  117.0 45.6 %all-to-all-done = bf16[16,64,1024]{2,1,0:T(8,128)(2,1)S(1)} async-done(((bf16[16,64,1024]{2,1,0:T(8,128)(2,1)}), bf16[16,64,1024]{2,1,0:T(8,128)(2,1)S(1)}, u32[]{:S(2)}, u32[]{:S(2)}) %all-to-all-start) | async-done | bytes 2097184 | tf_op jit(solution)/shard_map/all_to_all | solution.py:17
  162.7 0.8 fusion.34
  163.6 0.7 fusion.28
  164.5 0.7 fusion.25
  165.4 0.7 fusion.23
  166.2 0.6 fusion.13
  166.8 0.9 copy.21
  168.2 3.8 %reduce = bf16[1024,256]{1,0:T(8,128)(2,1)S(1)} reduce(bf16[1024,1,256]{2,1,0:T(2,128)(2,1)S(1)} %bitcast.64, bf16[]{:T(256)} %broadcast.24), dimensions={1}, to_apply=%bitcast.51.reduce_sub_computation | reduce | bytes 1048578
  172.0 0.9 reshape.124
  172.9 6.4 %all-to-all-start.1 = ((bf16[16,2,8192]{2,1,0:T(2,128)(2,1)}), bf16[16,2,8192]{2,1,0:T(2,128)(2,1)S(1)}, u32[]{:S(2)}, u32[]{:S(2)}) async-start(bf16[16,2,8192]{2,1,0:T(2,128)(2,1)} %reshape.124), calls=%async_computation.1 | async-start | bytes 1048576 | tf_op jit(solution)/shard_map/all_to_all | solution.py:40
  179.4 13.3 %all-to-all-done.1 = bf16[16,2,8192]{2,1,0:T(2,128)(2,1)S(1)} async-done(((bf16[16,2,8192]{2,1,0:T(2,128)(2,1)}), bf16[16,2,8192]{2,1,0:T(2,128)(2,1)S(1)}, u32[]{:S(2)}, u32[]{:S(2)}) %all-to-all-start.1) | async-done | bytes 524320 | tf_op jit(solution)/shard_map/all_to_all | solution.py:40
  192.8 0.5 reshape.125
  193.3 3.3 convolution_convert_fusion.1
  196.6 7.8 %reshape_reshape.3 = bf16[16,64,2,1024]{3,2,1,0:T(2,128)(2,1)} reshape(bf16[1024,2048]{1,0:T(8,128)(2,1)} %convolution_convert_fusion.1) | data formatting | bytes 8388608 | tf_op jit(solution)/shard_map/reshape;reshape | solution.py:47
  204.4 80.0 %fusion.5 = f32[16,2,512]{2,0,1:T(8,128)} fusion(bf16[512,64,1024]{2,1,0:T(8,128)(2,1)} %param.5, bf16[16,64,2,1024]{3,2,1,0:T(2,128)(2,1)} %reshape_reshape.3), kind=kOutput, calls=%fused_computation.7 | convolution fusion | flops 2147483648 | bytes 71368704 | tf_op jit(solution)/shard_map/dot_general | solution.py:51
  284.4 1.0 copy.24
  285.4 35.9 %all-gather.4.cloned.1.call-done = f32[256,2,512]{2,0,1:T(8,128)} async-done(((f32[16,2,512]{2,0,1:T(8,128)}), f32[256,2,512]{2,0,1:T(8,128)}) %all-gather.4.cloned.1.call-update) | async-done | bytes 1048592 | tf_op jit(solution)/shard_map/all_gather | solution.py:54
  321.3 1.3 reduce_sum.9
  322.6 0.6 copy.25
  (18 shorter events, 1.4 us)
Async XLA Ops:
  7.2 58.6 %copy-start.2 = (bf16[1,512]{1,0:T(2,128)(2,1)S(1)}, bf16[1,512]{1,0:T(2,128)(2,1)}, u32[]{:S(2)}) copy-start(bf16[1,512]{1,0:T(2,128)(2,1)} %param.4) | copy-start | bytes 3076
  109.9 6.9 %copy-start = (bf16[1,1024,256]{2,1,0:T(8,128)(2,1)S(1)}, bf16[1,1024,256]{2,1,0:T(8,128)(2,1)}, u32[]{:S(2)}) copy-start(bf16[1,1024,256]{2,1,0:T(8,128)(2,1)} %param.6) | copy-start | bytes 1572868
  109.9 52.8 %all-to-all-start = ((bf16[16,64,1024]{2,1,0:T(8,128)(2,1)}), bf16[16,64,1024]{2,1,0:T(8,128)(2,1)S(1)}, u32[]{:S(2)}, u32[]{:S(2)}) async-start(bf16[16,64,1024]{2,1,0:T(8,128)(2,1)} %bitcast.63), calls=%async_computation | async-start | bytes 4194304 | tf_op jit(solution)/shard_map/all_to_all | solution.py:17
  167.7 11.7 %copy-start.1 = (bf16[1024,256]{1,0:T(8,128)(2,1)S(1)}, bf16[1024,256]{1,0:T(8,128)(2,1)}, u32[]{:S(2)}) copy-start(bf16[1024,256]{1,0:T(8,128)(2,1)} %param.7) | copy-start | bytes 1572868
  172.9 19.8 %all-to-all-start.1 = ((bf16[16,2,8192]{2,1,0:T(2,128)(2,1)}), bf16[16,2,8192]{2,1,0:T(2,128)(2,1)S(1)}, u32[]{:S(2)}, u32[]{:S(2)}) async-start(bf16[16,2,8192]{2,1,0:T(2,128)(2,1)} %reshape.124), calls=%async_computation.1 | async-start | bytes 1048576 | tf_op jit(solution)/shard_map/all_to_all | solution.py:40
  179.3 142.0 %all-gather.4.cloned.1.call-start = ((), (), s32[]{:S(2)}) async-start(), calls=%async_computation.2 | async-start | bytes 1114112 | tf_op jit(solution)/shard_map/all_gather | solution.py:54
Sparse Core Ops, SparseCore 0:
  284.5 36.7 all-gather.3
